TPU v7x, 256 devices: a whole 4x4x8 slice. The times are simulated.
256 devices in a mesh: pole: 2 (over core), row: 4 (over y), col: 2 (over x_hi), layer: 16 (over z, x_lo).
Axes of the slice: x: 4 (x_hi: 2, x_lo: 2; x = x_hi * 2 + x_lo), y: 4, z: 8, core: 2. Of those that a mesh axis runs over, the one named last changes fastest.
Arguments:
- hamilton: bfloat16 [4096, 4096], P('layer', ('row', 'col')), may hold values from -0.0014648438 to 0.0014648438
- intersection: bfloat16 [4096, 4096], P('layer', ('row', 'col')), may hold values from -0.0014648438 to 0.0014648438
- guess: bfloat16 [2, 2, 4096, 4096], P('pole', None, 'layer', ('row', 'col')), may hold values from -6 to 6
- poles: float32 [2, 2], P('pole'), may hold values from -1.5 to 1.5
- weights: float32 [2, 2], P('pole'), may hold values from -1 to 1
- keep: int32 [2, 32, 32], P('pole'), may hold values from 0 to 1, as said below
Outputs:
- density: float32 [16, 2, 128, 4096], P('layer', 'pole', None, ('row', 'col'))
Inputs may be any that keep to these rules, and one draw needn't show every extreme that they name: keep[p, i, j] is 1 where tile (i, j) survives pole p's filter and 0 where it is dropped; diagonal tiles are always kept.
All inputs are finite; a program needn't handle non-finite values.
Results may differ from a plain program's by a relative error of at most 0.0032.
Values may be sent and summed in bfloat16 or wider, within the bound.
No kernel may reach another device: no remote copies, remote signals or barrier semaphores. Data moves between devices by JAX's collectives and lax.ppermute only.
A program may use at most 64 MiB of HBM per device.

v0:
```python
import jax
import jax.numpy as jnp
from jax import lax
from jax.sharding import Mesh
from jax.sharding import PartitionSpec as P

BLOCK = 128
LAYER = ("layer_0", "layer_1")


def sent_together(arrays, axis, dim, along):
    both = jnp.concatenate(arrays, axis=along)
    whole, at, gathered = (lax.all_gather(both, axis, axis=dim, tiled=True), 0, [])
    for a in arrays:
        gathered.append(lax.slice_in_dim(whole, at, at + a.shape[along], axis=along))
        at += a.shape[along]
    return tuple(gathered)


def whole_of(shard, axes, dim):
    for axis in reversed(axes):
        shard = lax.all_gather(shard, axis, axis=dim, tiled=True)
    return shard


def in_blocks(shard, dim, count):
    lengths = shard.shape
    parts = shard.reshape(*lengths[:dim], count, lengths[dim] // count, *lengths[dim + 1 :])
    return jnp.moveaxis(parts, dim, 0)


def sum_at_owner(shard, axis, dim):
    count = lax.axis_size(axis)
    parts = lax.all_to_all(in_blocks(shard, dim, count), axis, 0, 0, tiled=True)
    return jnp.sum(parts, axis=0)


def tile_mask(keep_float, row_ids, col_ids):
    tile_count = keep_float.shape[0]
    tile_ids = jnp.arange(tile_count, dtype=jnp.int32)
    pick_rows = (row_ids[:, None] // BLOCK == tile_ids[None, :]).astype(jnp.float32)
    pick_cols = (col_ids[:, None] // BLOCK == tile_ids[None, :]).astype(jnp.float32)
    half_mask = jnp.dot(pick_rows, keep_float, precision=lax.Precision.HIGHEST)
    return jnp.dot(half_mask, pick_cols.T, precision=lax.Precision.HIGHEST)


def fold_terms(left_panel, piece):
    real_part = jnp.dot(left_panel[0], piece[0], preferred_element_type=jnp.float32) - jnp.dot(
        left_panel[1], piece[1], preferred_element_type=jnp.float32
    )
    imag_part = jnp.dot(left_panel[0], piece[1], preferred_element_type=jnp.float32) + jnp.dot(
        left_panel[1], piece[0], preferred_element_type=jnp.float32
    )
    return jnp.stack([real_part, imag_part])


def per_device(hamilton, intersection, guess, poles, weights, keep):
    rows_local, cols_local = hamilton.shape
    layer_index = lax.axis_index(LAYER)
    span_index = lax.axis_index("row") * lax.axis_size("col") + lax.axis_index("col")
    row_ids = layer_index * rows_local + jnp.arange(rows_local, dtype=jnp.int32)
    col_ids = span_index * cols_local + jnp.arange(cols_local, dtype=jnp.int32)
    ham_rows, ovl_rows = sent_together((hamilton, intersection), ("row", "col"), 1, 0)
    ham_wide = ham_rows.astype(jnp.float32)
    ovl_wide = ovl_rows.astype(jnp.float32)
    real_pole = poles[0, 0]
    imag_pole = poles[0, 1]
    system_panel = jnp.stack([real_pole * ovl_wide - ham_wide, imag_pole * ovl_wide]).astype(
        jnp.bfloat16
    )
    guess_local = guess[0]
    own_mask = tile_mask(keep[0].astype(jnp.float32), row_ids, col_ids)
    first = fold_terms(system_panel, whole_of(guess_local, LAYER, 1))
    product_local = (own_mask[None] * first).astype(jnp.bfloat16)
    guess_panel = lax.all_gather(guess_local, ("row", "col"), axis=2, tiled=True)
    back = fold_terms(guess_panel, lax.all_gather(product_local, LAYER, axis=1, tiled=True))
    refined = own_mask[None] * (2.0 * guess_local.astype(jnp.float32) - back)
    contrib = weights[0, 0] * refined[0] - weights[0, 1] * refined[1]
    reduced = sum_at_owner(contrib, "pole", 0)
    return reduced.reshape(1, 1, reduced.shape[0], cols_local)


def solution(mesh):
    split = Mesh(
        mesh.devices.reshape(mesh.shape["pole"], mesh.shape["row"], mesh.shape["col"], 8, 2),
        ("pole", "row", "col", "layer_0", "layer_1"),
    )
    return jax.shard_map(
        per_device,
        mesh=split,
        in_specs=(
            P(LAYER, ("row", "col")),
            P(LAYER, ("row", "col")),
            P("pole", None, LAYER, ("row", "col")),
            P("pole", None),
            P("pole", None),
            P("pole", None, None),
        ),
        out_specs=P(LAYER, "pole", None, ("row", "col")),
        check_vma=False,
    )
```

profile of v0, /device:TPU:1, one launch (start us, length us, event | category | flops | bytes accessed | tf_op | source)
XLA Modules:
  0.0 499.8 jit_solution(3519931919193923435)
XLA Ops:
  6.5 0.0 all-gather.13.cloned.1.call-start
  6.5 0.7 all-gather.13.cloned.1.call-update
  7.3 0.0 all-gather.9.cloned.1.call-start
  7.3 1.9 pad_maximum_fusion
  9.2 0.0 all-gather.9.cloned.1.call-update
  9.2 0.0 all-gather.15.cloned.1.call-start
  9.3 29.9 %all-gather.13.cloned.1.call-done = bf16[1,2,512,512]{3,2,1,0:T(8,128)(2,1)} async-done(((bf16[1,2,256,512]{3,2,1,0:T(8,128)(2,1)}), bf16[1,2,512,512]{3,2,1,0:T(8,128)(2,1)}) %all-gather.13.cloned.1.call-update) | async-done | bytes 1048592 | tf_op jit(solution)/shard_map/all_gather | solution.py:22
  39.1 0.0 all-gather.15.cloned.1.call-update
  39.2 0.0 all-gather.17.cloned.1.call-start
  39.2 0.5 all-gather.17.cloned.1.call-update
  39.7 0.0 all-gather.11.cloned.1.call-start
  39.8 1.4 fusion.40
  41.2 1.0 fusion.30
  42.2 0.5 fusion.28
  42.7 77.4 %all-gather.9.cloned.1.call-done = bf16[512,4096]{1,0:T(8,128)(2,1)} async-done(((bf16[512,512]{1,0:T(8,128)(2,1)}), bf16[512,4096]{1,0:T(8,128)(2,1)}) %all-gather.9.cloned.1.call-update) | async-done | bytes 4194320 | tf_op jit(solution)/shard_map/all_gather | solution.py:13
  120.1 94.4 %all-gather.15.cloned.1.call-done = bf16[1,2,4096,512]{3,2,1,0:T(8,128)(2,1)} async-done(((bf16[1,2,512,512]{3,2,1,0:T(8,128)(2,1)}), bf16[1,2,4096,512]{3,2,1,0:T(8,128)(2,1)}) %all-gather.15.cloned.1.call-update) | async-done | bytes 8388624 | tf_op jit(solution)/shard_map/all_gather | solution.py:22
  214.5 0.0 copy-start.2
  214.5 5.0 %fusion.3 = f32[256,512]{1,0:T(8,128)S(1)} fusion(bf16[1,2,4096,512]{3,2,1,0:T(8,128)(2,1)} %all-gather.15.cloned.1.call-done, f32[]{:T(128)} %bitcast.5, bf16[512,4096]{1,0:T(8,128)(2,1)} %all-gather.9.cloned.1.call-done), kind=kOutput, calls=%fused_computation.9 | convolution fusion | flops 1076887552 | bytes 6816256 | tf_op jit(solution)/shard_map/dot_general | solution.py:51
  219.5 0.2 copy-done.2
  219.7 0.0 copy-start.5
  219.7 4.5 fusion.4
  224.2 0.0 copy-done.5
  224.2 1.9 fusion.20
  226.1 0.0 copy-start.1
  226.1 1.9 fusion.24
  228.1 1.0 fusion.25
  229.1 0.0 all-gather.11.cloned.1.call-update
  229.1 0.0 copy-done.1
  229.1 0.6 fusion.39
  229.8 63.1 %all-gather.17.cloned.1.call-done = bf16[1,2,256,4096]{3,2,1,0:T(8,128)(2,1)} async-done(((bf16[1,2,256,512]{3,2,1,0:T(8,128)(2,1)}), bf16[1,2,256,4096]{3,2,1,0:T(8,128)(2,1)}) %all-gather.17.cloned.1.call-update) | async-done | bytes 4194320 | tf_op jit(solution)/shard_map/all_gather | solution.py:75
  292.9 182.6 %all-gather.11.cloned.1.call-done = bf16[2,4096,512]{2,1,0:T(8,128)(2,1)} async-done(((bf16[2,256,512]{2,1,0:T(8,128)(2,1)}), bf16[2,4096,512]{2,1,0:T(8,128)(2,1)}) %all-gather.11.cloned.1.call-update) | async-done | bytes 8388624 | tf_op jit(solution)/shard_map/all_gather | solution.py:76
  475.5 0.0 copy-start.3
  475.5 4.2 fusion.7
  479.7 1.0 copy-done.3
  480.7 0.0 copy-start.4
  480.7 3.0 fusion.8
  483.7 0.0 copy-done.4
  483.7 1.2 fusion.16
  485.0 0.0 copy-start
  485.0 1.2 fusion.14
  486.3 0.0 copy-done
  486.3 0.2 fusion.26
  486.5 1.4 fusion.27
  487.9 4.6 all_to_all.5
  492.6 0.7 reduce_sum.9
  (2 shorter events, 0.0 us)
Async XLA Ops:
  6.5 32.6 %all-gather.13.cloned.1.call-start = ((), (), s32[]{:S(2)}) async-start(), calls=%async_computation.3 | async-start | bytes 1572864 | tf_op jit(solution)/shard_map/all_gather | solution.py:22
  7.3 112.8 %all-gather.9.cloned.1.call-start = ((), (), s32[]{:S(2)}) async-start(), calls=%async_computation.1 | async-start | bytes 4718592 | tf_op jit(solution)/shard_map/all_gather | solution.py:13
  9.2 205.3 %all-gather.15.cloned.1.call-start = ((), (), s32[]{:S(2)}) async-start(), calls=%async_computation.4 | async-start | bytes 9437184 | tf_op jit(solution)/shard_map/all_gather | solution.py:22
  39.2 253.7 %all-gather.17.cloned.1.call-start = ((), (), s32[]{:S(2)}) async-start(), calls=%async_computation.5 | async-start | bytes 4718592 | tf_op jit(solution)/shard_map/all_gather | solution.py:75
  39.7 435.7 %all-gather.11.cloned.1.call-start = ((), (), s32[]{:S(2)}) async-start(), calls=%async_computation.2 | async-start | bytes 8912896 | tf_op jit(solution)/shard_map/all_gather | solution.py:76
  214.5 5.2 %copy-start.2 = (bf16[1,2,4096,512]{3,2,1,0:T(8,128)(2,1)S(1)}, bf16[1,2,4096,512]{3,2,1,0:T(8,128)(2,1)}, u32[]{:S(2)}) copy-start(bf16[1,2,4096,512]{3,2,1,0:T(8,128)(2,1)} %all-gather.15.cloned.1.call-done) | copy-start | bytes 25165828
  219.7 4.5 copy-start.5
  226.1 3.0 copy-start.1
  475.5 5.2 %copy-start.3 = (bf16[2,4096,512]{2,1,0:T(8,128)(2,1)S(1)}, bf16[2,4096,512]{2,1,0:T(8,128)(2,1)}, u32[]{:S(2)}) copy-start(bf16[2,4096,512]{2,1,0:T(8,128)(2,1)} %all-gather.11.cloned.1.call-done) | copy-start | bytes 25165828
  480.7 3.0 copy-start.4
  485.0 1.3 copy-start
Sparse Core Ops, SparseCore 0:
  9.1 29.9 all-gather.12
  41.6 78.4 all-gather.8
  121.9 92.5 all-gather.14
  216.8 76.0 all-gather.16
  294.5 180.8 all-gather.10
where the time goes:
time: 500 us
  waiting for transfers between devices  449 us (90%)
  matrix products  24.5 us (5%)
  between operations  13.3 us (3%)
  other arithmetic  5.32 us (1%)
    all_gather x1, waiting for transfers between devices, per_device(): lax.all_gather(product_local, LAYER, axis=1, tiled=True)  183 us
    all_gather x2, waiting for transfers between devices, whole_of(): shard = lax.all_gather(shard, axis, axis=dim, tiled=True)  124 us
    all_gather x1, waiting for transfers between devices, sent_together(): lax.all_gather(both, axis, axis=dim, tiled=True)  77.4 us
    all_gather x1, waiting for transfers between devices, per_device(): lax.all_gather(guess_local, ('row', 'col'), axis=2, tiled=True)  63.1 us
  transfers between devices with their start and end apart: 5, of which 5 were waited for; matrix products, arithmetic and copies ran while one was open for 4% of the time, Pallas kernels for 0%

commit v1 on v0

--- a/solution.py
+++ b/solution.py
@@ -6,6 +6,11 @@
 
 BLOCK = 128
 LAYER = ("layer_0", "layer_1")
+
+
+def swapped_in(shard, name, d):
+    stack = jnp.stack([shard] * lax.axis_size(name))
+    return jnp.concatenate(lax.all_to_all(stack, name, 0, 0), axis=d)
 
 
 def sent_together(arrays, axis, dim, along):
@@ -73,7 +78,7 @@
     first = fold_terms(system_panel, whole_of(guess_local, LAYER, 1))
     product_local = (own_mask[None] * first).astype(jnp.bfloat16)
     guess_panel = lax.all_gather(guess_local, ("row", "col"), axis=2, tiled=True)
-    back = fold_terms(guess_panel, lax.all_gather(product_local, LAYER, axis=1, tiled=True))
+    back = fold_terms(guess_panel, swapped_in(product_local, LAYER, 1))
     refined = own_mask[None] * (2.0 * guess_local.astype(jnp.float32) - back)
     contrib = weights[0, 0] * refined[0] - weights[0, 1] * refined[1]
     reduced = sum_at_owner(contrib, "pole", 0)

time: 500 us -> 459 us (0.918)
  waiting for transfers between devices: 449 us -> 394 us
  local copies, waits for them, and re-layouts: 3.25 us -> 14 us
  starting transfers between devices: 0.16 us -> 5.36 us
    all_to_all x0 -> x1, waiting for transfers between devices: none -> 190 us  [swapped_in(): return jnp.concatenate(lax.all_to_all(stack, name, 0, 0), axis=d)]
    all_gather x1 -> x0, waiting for transfers between devices: 183 us -> none  [per_device(): lax.all_gather(product_local, LAYER, axis=1, tiled=True)]
    all_gather x1, waiting for transfers between devices: 63.1 us -> 0.01 us  [per_device(): lax.all_gather(guess_local, ('row', 'col'), axis=2, tiled=True)]
    slice x0 -> x1, local copies, waits for them, and re-layouts: none -> 5.81 us  [fold_terms(): piece[0]]
    all_to_all x0 -> x1, starting transfers between devices: none -> 5.23 us  [swapped_in(): return jnp.concatenate(lax.all_to_all(stack, name, 0, 0), axis=d)]
  transfers between devices with their start and end apart: 5 -> 5, of which waited for: 5 -> 4; matrix products, arithmetic and copies ran while one was open for 4% -> 2% of each run, Pallas kernels for 0% -> 0%
where the time goes in v1:
time: 459 us
  waiting for transfers between devices  394 us (86%)
  matrix products  22.6 us (5%)
  local copies, waits for them, and re-layouts  14 us (3%)
  between operations  13.3 us (3%)
  starting transfers between devices  5.36 us (1%)
  blocking collectives  5.24 us (1%)
    all_to_all x1, waiting for transfers between devices, swapped_in(): return jnp.concatenate(lax.all_to_all(stack, name, 0, 0), axis=d)  190 us
    all_gather x2, waiting for transfers between devices, whole_of(): shard = lax.all_gather(shard, axis, axis=dim, tiled=True)  124 us
    all_gather x1, waiting for transfers between devices, sent_together(): lax.all_gather(both, axis, axis=dim, tiled=True)  78 us
    dot_general x2, matrix products, fold_terms(): jnp.dot(left_panel[0], piece[0], preferred_element_type=jnp.float32)  10 us
  transfers between devices with their start and end apart: 5, of which 4 were waited for; matrix products, arithmetic and copies ran while one was open for 2% of the time, Pallas kernels for 0%

profile of v1, /device:TPU:1, one launch (start us, length us, event | category | flops | bytes accessed | tf_op | source)
XLA Modules:
  0.0 458.6 jit_solution(951863874355902365)
XLA Ops:
  6.5 0.0 all-gather.10.cloned.1.call-start
  6.5 0.7 all-gather.10.cloned.1.call-update
  7.3 0.0 all-gather.8.cloned.1.call-start
  7.3 1.9 pad_maximum_fusion
  9.2 0.0 all-gather.8.cloned.1.call-update
  9.2 0.0 all-gather.12.cloned.1.call-start
  9.2 29.9 %all-gather.10.cloned.1.call-done = bf16[1,2,512,512]{3,2,1,0:T(8,128)(2,1)} async-done(((bf16[1,2,256,512]{3,2,1,0:T(8,128)(2,1)}), bf16[1,2,512,512]{3,2,1,0:T(8,128)(2,1)}) %all-gather.10.cloned.1.call-update) | async-done | bytes 1048592 | tf_op jit(solution)/shard_map/all_gather | solution.py:27
  39.1 0.0 all-gather.12.cloned.1.call-update
  39.2 1.4 fusion.41
  40.6 1.0 fusion.30
  41.6 0.5 fusion.28
  42.1 78.0 %all-gather.8.cloned.1.call-done = bf16[512,4096]{1,0:T(8,128)(2,1)} async-done(((bf16[512,512]{1,0:T(8,128)(2,1)}), bf16[512,4096]{1,0:T(8,128)(2,1)}) %all-gather.8.cloned.1.call-update) | async-done | bytes 4194320 | tf_op jit(solution)/shard_map/all_gather | solution.py:18
  120.1 94.4 %all-gather.12.cloned.1.call-done = bf16[1,2,4096,512]{3,2,1,0:T(8,128)(2,1)} async-done(((bf16[1,2,512,512]{3,2,1,0:T(8,128)(2,1)}), bf16[1,2,4096,512]{3,2,1,0:T(8,128)(2,1)}) %all-gather.12.cloned.1.call-update) | async-done | bytes 8388624 | tf_op jit(solution)/shard_map/all_gather | solution.py:27
  214.5 0.0 copy-start.4
  214.5 0.0 copy-start.5
  214.5 5.8 %fusion.4 = f32[256,512]{1,0:T(8,128)S(1)} fusion(bf16[1,2,4096,512]{3,2,1,0:T(8,128)(2,1)} %all-gather.12.cloned.1.call-done, bf16[512,4096]{1,0:T(8,128)(2,1)} %all-gather.8.cloned.1.call-done, f32[]{:T(128)} %bitcast.3), kind=kOutput, calls=%fused_computation.8 | convolution fusion | flops 1078984704 | bytes 8913408 | tf_op jit(solution)/shard_map/dot_general | solution.py:53
  220.3 0.0 copy-done.4
  220.3 1.2 copy-done.5
  221.5 1.9 fusion.3
  223.4 1.9 fusion.16
  225.3 1.9 fusion.20
  227.2 0.2 fusion.25
  227.4 4.2 stack.20
  231.6 0.0 copy-start.3
  231.6 5.2 %all-to-all-start = ((bf16[16,2,256,512]{3,2,1,0:T(8,128)(2,1)}), bf16[16,2,256,512]{3,2,1,0:T(8,128)(2,1)}, u32[]{:S(2)}, u32[]{:S(2)}) async-start(bf16[16,2,256,512]{3,2,1,0:T(8,128)(2,1)} %stack.20), calls=%async_computation | async-start | bytes 16777216 | tf_op jit(solution)/shard_map/all_to_all | solution.py:13
  236.8 0.0 all-gather.14.cloned.1.call-start
  236.9 0.5 all-gather.14.cloned.1.call-update
  237.4 0.0 copy-done.3
  237.4 0.6 fusion.40
  238.0 190.1 %all-to-all-done = bf16[16,2,256,512]{3,2,1,0:T(8,128)(2,1)} async-done(((bf16[16,2,256,512]{3,2,1,0:T(8,128)(2,1)}), bf16[16,2,256,512]{3,2,1,0:T(8,128)(2,1)}, u32[]{:S(2)}, u32[]{:S(2)}) %all-to-all-start) | async-done | bytes 8388640 | tf_op jit(solution)/shard_map/all_to_all | solution.py:13
  428.1 5.8 %fusion.39 = (bf16[1,16,256,512]{3,2,0,1:T(8,128)(2,1)}, bf16[1,16,256,512]{3,2,0,1:T(8,128)(2,1)}) fusion(bf16[2,16,256,512]{3,2,0,1:T(8,128)(2,1)} %bitcast.9), kind=kLoop, calls=%fused_computation.54 | loop fusion | bytes 16777216 | tf_op jit(solution)/shard_map/slice | solution.py:53
  433.9 0.0 all-gather.14.cloned.1.call-done
  433.9 0.0 copy-start.2
  433.9 4.2 fusion.7
  438.1 0.0 copy-start.6
  438.1 0.0 copy-done.2
  438.1 3.0 fusion.8
  441.1 0.0 copy-done.6
  441.1 0.0 copy-start.1
  441.1 1.2 fusion.24
  442.4 0.9 copy-done.1
  443.3 0.0 copy-start
  443.3 1.2 fusion.22
  444.6 0.0 copy-done
  444.6 0.2 fusion.26
  444.8 1.3 fusion.27
  446.1 5.2 %all_to_all.10 = f32[2,128,512]{2,1,0:T(8,128)S(1)} all-to-all(f32[2,128,512]{2,1,0:T(8,128)S(1)} %bitcast.67), channel_id=1, replica_groups=mesh['pole'=2,'row'=4,'col'=2,'layer_0'=8,'layer_1'=2] {'pole'}, dimensions={0} | all-to-all | bytes 1048576 | tf_op jit(solution)/shard_map/all_to_all | solution.py:39
  451.3 0.7 reduce_sum.9
  (2 shorter events, 0.0 us)
Async XLA Ops:
  6.5 32.6 %all-gather.10.cloned.1.call-start = ((), (), s32[]{:S(2)}) async-start(), calls=%async_computation.3 | async-start | bytes 1572864 | tf_op jit(solution)/shard_map/all_gather | solution.py:27
  7.3 112.8 %all-gather.8.cloned.1.call-start = ((), (), s32[]{:S(2)}) async-start(), calls=%async_computation.2 | async-start | bytes 4718592 | tf_op jit(solution)/shard_map/all_gather | solution.py:18
  9.2 205.3 %all-gather.12.cloned.1.call-start = ((), (), s32[]{:S(2)}) async-start(), calls=%async_computation.4 | async-start | bytes 9437184 | tf_op jit(solution)/shard_map/all_gather | solution.py:27
  214.5 5.9 %copy-start.4 = (bf16[1,2,4096,512]{3,2,1,0:T(8,128)(2,1)S(1)}, bf16[1,2,4096,512]{3,2,1,0:T(8,128)(2,1)}, u32[]{:S(2)}) copy-start(bf16[1,2,4096,512]{3,2,1,0:T(8,128)(2,1)} %all-gather.12.cloned.1.call-done) | copy-start | bytes 25165828
  214.5 7.0 %copy-start.5 = (bf16[512,4096]{1,0:T(8,128)(2,1)S(1)}, bf16[512,4096]{1,0:T(8,128)(2,1)}, u32[]{:S(2)}) copy-start(bf16[512,4096]{1,0:T(8,128)(2,1)} %all-gather.8.cloned.1.call-done) | copy-start | bytes 12582916
  231.6 5.8 %copy-start.3 = (f32[1,2]{1,0:T(1,128)S(1)}, f32[1,2]{1,0:T(1,128)}, u32[]{:S(2)}) copy-start(f32[1,2]{1,0:T(1,128)} %param.10) | copy-start | bytes 28
  231.6 196.5 %all-to-all-start = ((bf16[16,2,256,512]{3,2,1,0:T(8,128)(2,1)}), bf16[16,2,256,512]{3,2,1,0:T(8,128)(2,1)}, u32[]{:S(2)}, u32[]{:S(2)}) async-start(bf16[16,2,256,512]{3,2,1,0:T(8,128)(2,1)} %stack.20), calls=%async_computation | async-start | bytes 16777216 | tf_op jit(solution)/shard_map/all_to_all | solution.py:13
  236.8 197.0 %all-gather.14.cloned.1.call-start = ((), (), s32[]{:S(2)}) async-start(), calls=%async_computation.5 | async-start | bytes 4718592 | tf_op jit(solution)/shard_map/all_gather | solution.py:80
  433.9 4.2 copy-start.2
  438.1 3.0 copy-start.6
  441.1 2.2 copy-start.1
  443.3 1.3 copy-start
Sparse Core Ops, SparseCore 0:
  9.1 29.9 all-gather.9
  41.6 78.4 all-gather.7
  121.9 92.5 all-gather.11
  239.8 79.7 all-gather.13
